TPU v7x, 32 devices: a whole 2x2x4 slice. The times are simulated.
32 devices in a mesh: gx: 8 (over z, x), af: 4 (over y, core).
Axes of the slice: x: 2, y: 2, z: 4, core: 2. Of those that a mesh axis runs over, the one named last changes fastest.
Arguments:
- forcing: float32 [16, 2, 32, 5, 4, 256], P('af', None, 'gx'), may hold values from -6 to 6
- flow: float32 [32, 4, 256], P('gx'), may hold values from 0.2 to 1
- sponge: float32 [32, 4, 256], P('gx'), may hold values from 0.05 to 0.5
- coupling: float32 [5, 5], replicated, may hold values from -1.5 to 1.5
- omega: float32 [2], replicated, may hold values from 1 to 1.6
Outputs:
- basis: float32 [16, 2, 32, 5, 4, 256], P('af', None, 'gx')
- coeff: float32 [16, 16], replicated
All inputs are finite; a program needn't handle non-finite values.
Results may differ from a plain program's by a relative error of at most 0.0001.
Values sent between devices are 32-bit elements; how exact they have to be, the bound alone decides.
No kernel may reach another device: no remote copies, remote signals or barrier semaphores. Data moves between devices by JAX's collectives and lax.ppermute only.
A program may use at most 64 MiB of HBM per device.

v0:
```python
import jax
import jax.numpy as jnp
from jax import lax
from jax.sharding import PartitionSpec as P

FORCINGS = 8
SWEEPS = 8
viscosity = 0.25


def padded_2(array, sides, width):
    for axis, dim in sides:
        size, length = (lax.axis_size(axis), array.shape[dim])
        up = [(i, (i + 1) % size) for i in range(size - 1)]
        down = [(j, i) for i, j in up]
        last = lax.slice_in_dim(array, length - width, length, axis=dim)
        leading = lax.slice_in_dim(array, 0, width, axis=dim)
        before = lax.ppermute(last, axis, up)
        after = lax.ppermute(leading, axis, down)
        array = jnp.concatenate([before, array, after], axis=dim)
    return array


def apply_adjoint(padded, freq, flow, sponge, coupling):
    field = padded[:, :, 1:-1]
    upper = padded[:, :, 2:]
    lower = padded[:, :, :-2]
    radial = jnp.pad(field, ((0, 0), (0, 0), (0, 0), (0, 0), (1, 1), (0, 0)))
    lap = upper + lower + radial[:, :, :, :, 2:, :] + radial[:, :, :, :, :-2, :]
    lap = lap + jnp.roll(field, 1, -1) + jnp.roll(field, -1, -1) - 6.0 * field
    advect = 0.5 * flow[None, None, :, None] * (lower - upper)
    mixed = jnp.einsum("wv,kpxwrt->kpxvrt", coupling, field, precision=lax.Precision.HIGHEST)
    rotate = jnp.stack([freq * field[:, 1], -freq * field[:, 0]], axis=1)
    return sponge[None, None, :, None] * field + rotate - mixed + advect - viscosity * lap


def precondition(resid, freq, sponge, coupling):
    diag_re = sponge[:, None] + 6.0 * viscosity - jnp.diagonal(coupling)[None, :, None, None]
    diag_re = diag_re[None]
    denom = diag_re * diag_re + freq * freq
    p_re = diag_re / denom
    p_im = freq / denom
    part_re = p_re * resid[:, 0] - p_im * resid[:, 1]
    part_im = p_re * resid[:, 1] + p_im * resid[:, 0]
    return jnp.stack([part_re, part_im], axis=1)


def with_faces(field):
    return padded_2(field, (("gx", 2),), 1)


def on_device(forcing, flow, sponge, coupling, omega):
    local_cols = forcing.shape[0]
    column_ids = lax.axis_index("af") * local_cols + jnp.arange(local_cols)
    freq_vec = jnp.where(column_ids < FORCINGS, omega[0], omega[1])
    freq_b = freq_vec[:, None, None, None, None]
    field = precondition(forcing, freq_b, sponge, coupling)
    for sweep in range(SWEEPS):
        padded = with_faces(field)
        image = apply_adjoint(padded, freq_b, flow, sponge, coupling)
        field = field + precondition(forcing - image, freq_b, sponge, coupling)
    all_cols = local_cols * lax.axis_size("af")
    eye_matrix = jnp.eye(all_cols, dtype=jnp.float32)
    regrouped = lax.all_to_all(field, "af", split_axis=4, concat_axis=0, tiled=True)
    flat = regrouped.reshape(all_cols, -1)
    total = flat.shape[1] * lax.axis_size("gx") * lax.axis_size("af")
    local_gram = jnp.dot(flat, flat.T, precision=lax.Precision.HIGHEST)
    partial_gram = lax.psum(local_gram, "af")
    gram = lax.psum(partial_gram, "gx")
    lower_factor = jnp.linalg.cholesky(gram)
    inverse = jax.scipy.linalg.solve_triangular(lower_factor, eye_matrix, lower=True)
    scaled = jnp.dot(inverse, flat, precision=lax.Precision.HIGHEST) * jnp.sqrt(jnp.float32(total))
    basis = lax.all_to_all(
        scaled.reshape(regrouped.shape), "af", split_axis=0, concat_axis=4, tiled=True
    )
    coeff = lower_factor.T / jnp.sqrt(jnp.float32(total))
    return (basis, coeff)


def solution(mesh):
    placed = (
        P("af", None, "gx", None, None, None),
        P("gx", None, None),
        P("gx", None, None),
        P(),
        P(),
    )
    return jax.shard_map(
        on_device,
        mesh=mesh,
        in_specs=placed,
        out_specs=(P("af", None, "gx", None, None, None), P()),
        check_vma=False,
    )
```

profile of v0, /device:TPU:0, one launch (start us, length us, event | category | flops | bytes accessed | tf_op | source)
XLA Modules:
  0.0 230.4 jit_solution(16400706654534699275)
XLA Ops:
  7.8 5.5 %collective-permute-start = (f32[4,2,1,5,4,256]{5,3,4,2,1,0:T(8,128)S(1)}, f32[4,2,1,5,4,256]{5,3,4,2,1,0:T(8,128)S(1)}, u32[]{:S(2)}, u32[]{:S(2)}) collective-permute-start(f32[4,2,1,5,4,256]{5,3,4,2,1,0:T(8,128)S(1)} %get-tuple-element.89), channel_id=1, source_target_pairs={{0,4},{4,8},{8,12},{12,16},{16,20},{20,24},{24,28},{1,5},{5,9},{9,... | collective-permute-start | bytes 491528 | tf_op jit(solution)/shard_map/ppermute | solution.py:18
  17.6 5.8 %collective-permute-done = f32[4,2,1,5,4,256]{5,3,4,2,1,0:T(8,128)S(1)} collective-permute-done((f32[4,2,1,5,4,256]{5,3,4,2,1,0:T(8,128)S(1)}, f32[4,2,1,5,4,256]{5,3,4,2,1,0:T(8,128)S(1)}, u32[]{:S(2)}, u32[]{:S(2)}) %collective-permute-start) | collective-permute-done | bytes 163872 | tf_op jit(solution)/shard_map/ppermute | solution.py:18
  27.9 5.0 %collective-permute-start.2 = (f32[4,2,1,5,4,256]{5,3,4,2,1,0:T(8,128)S(1)}, f32[4,2,1,5,4,256]{5,3,4,2,1,0:T(8,128)S(1)}, u32[]{:S(2)}, u32[]{:S(2)}) collective-permute-start(f32[4,2,1,5,4,256]{5,3,4,2,1,0:T(8,128)S(1)} %get-tuple-element.83), channel_id=1, source_target_pairs={{0,4},{4,8},{8,12},{12,16},{16,20},{20,24},{24,28},{1,5},{5,9},{9,... | collective-permute-start | bytes 491528 | tf_op jit(solution)/shard_map/ppermute | solution.py:18
  37.5 5.8 %collective-permute-done.2 = f32[4,2,1,5,4,256]{5,3,4,2,1,0:T(8,128)S(1)} collective-permute-done((f32[4,2,1,5,4,256]{5,3,4,2,1,0:T(8,128)S(1)}, f32[4,2,1,5,4,256]{5,3,4,2,1,0:T(8,128)S(1)}, u32[]{:S(2)}, u32[]{:S(2)}) %collective-permute-start.2) | collective-permute-done | bytes 163872 | tf_op jit(solution)/shard_map/ppermute | solution.py:18
  47.9 5.0 %collective-permute-start.4 = (f32[4,2,1,5,4,256]{5,3,4,2,1,0:T(8,128)S(1)}, f32[4,2,1,5,4,256]{5,3,4,2,1,0:T(8,128)S(1)}, u32[]{:S(2)}, u32[]{:S(2)}) collective-permute-start(f32[4,2,1,5,4,256]{5,3,4,2,1,0:T(8,128)S(1)} %get-tuple-element.75), channel_id=1, source_target_pairs={{0,4},{4,8},{8,12},{12,16},{16,20},{20,24},{24,28},{1,5},{5,9},{9,... | collective-permute-start | bytes 491528 | tf_op jit(solution)/shard_map/ppermute | solution.py:18
  53.1 4.3 %collective-permute-done.5 = f32[4,2,1,5,4,256]{5,3,4,2,1,0:T(8,128)S(1)} collective-permute-done((f32[4,2,1,5,4,256]{5,3,4,2,1,0:T(8,128)S(1)}, f32[4,2,1,5,4,256]{5,3,4,2,1,0:T(8,128)S(1)}, u32[]{:S(2)}, u32[]{:S(2)}) %collective-permute-start.5) | collective-permute-done | bytes 163872 | tf_op jit(solution)/shard_map/ppermute | solution.py:19
  57.5 5.8 %collective-permute-done.4 = f32[4,2,1,5,4,256]{5,3,4,2,1,0:T(8,128)S(1)} collective-permute-done((f32[4,2,1,5,4,256]{5,3,4,2,1,0:T(8,128)S(1)}, f32[4,2,1,5,4,256]{5,3,4,2,1,0:T(8,128)S(1)}, u32[]{:S(2)}, u32[]{:S(2)}) %collective-permute-start.4) | collective-permute-done | bytes 163872 | tf_op jit(solution)/shard_map/ppermute | solution.py:18
  68.0 5.2 %collective-permute-start.6 = (f32[4,2,1,5,4,256]{5,3,4,2,1,0:T(8,128)S(1)}, f32[4,2,1,5,4,256]{5,3,4,2,1,0:T(8,128)S(1)}, u32[]{:S(2)}, u32[]{:S(2)}) collective-permute-start(f32[4,2,1,5,4,256]{5,3,4,2,1,0:T(8,128)S(1)} %get-tuple-element.67), channel_id=1, source_target_pairs={{0,4},{4,8},{8,12},{12,16},{16,20},{20,24},{24,28},{1,5},{5,9},{9,... | collective-permute-start | bytes 491528 | tf_op jit(solution)/shard_map/ppermute | solution.py:18
  77.6 5.8 %collective-permute-done.6 = f32[4,2,1,5,4,256]{5,3,4,2,1,0:T(8,128)S(1)} collective-permute-done((f32[4,2,1,5,4,256]{5,3,4,2,1,0:T(8,128)S(1)}, f32[4,2,1,5,4,256]{5,3,4,2,1,0:T(8,128)S(1)}, u32[]{:S(2)}, u32[]{:S(2)}) %collective-permute-start.6) | collective-permute-done | bytes 163872 | tf_op jit(solution)/shard_map/ppermute | solution.py:18
  88.2 5.0 %collective-permute-start.8 = (f32[4,2,1,5,4,256]{5,3,4,2,1,0:T(8,128)S(1)}, f32[4,2,1,5,4,256]{5,3,4,2,1,0:T(8,128)S(1)}, u32[]{:S(2)}, u32[]{:S(2)}) collective-permute-start(f32[4,2,1,5,4,256]{5,3,4,2,1,0:T(8,128)S(1)} %get-tuple-element.59), channel_id=1, source_target_pairs={{0,4},{4,8},{8,12},{12,16},{16,20},{20,24},{24,28},{1,5},{5,9},{9,... | collective-permute-start | bytes 491528 | tf_op jit(solution)/shard_map/ppermute | solution.py:18
  93.5 4.3 %collective-permute-done.9 = f32[4,2,1,5,4,256]{5,3,4,2,1,0:T(8,128)S(1)} collective-permute-done((f32[4,2,1,5,4,256]{5,3,4,2,1,0:T(8,128)S(1)}, f32[4,2,1,5,4,256]{5,3,4,2,1,0:T(8,128)S(1)}, u32[]{:S(2)}, u32[]{:S(2)}) %collective-permute-start.9) | collective-permute-done | bytes 163872 | tf_op jit(solution)/shard_map/ppermute | solution.py:19
  97.8 5.8 %collective-permute-done.8 = f32[4,2,1,5,4,256]{5,3,4,2,1,0:T(8,128)S(1)} collective-permute-done((f32[4,2,1,5,4,256]{5,3,4,2,1,0:T(8,128)S(1)}, f32[4,2,1,5,4,256]{5,3,4,2,1,0:T(8,128)S(1)}, u32[]{:S(2)}, u32[]{:S(2)}) %collective-permute-start.8) | collective-permute-done | bytes 163872 | tf_op jit(solution)/shard_map/ppermute | solution.py:18
  108.6 5.0 %collective-permute-start.10 = (f32[4,2,1,5,4,256]{5,3,4,2,1,0:T(8,128)S(1)}, f32[4,2,1,5,4,256]{5,3,4,2,1,0:T(8,128)S(1)}, u32[]{:S(2)}, u32[]{:S(2)}) collective-permute-start(f32[4,2,1,5,4,256]{5,3,4,2,1,0:T(8,128)S(1)} %get-tuple-element.51), channel_id=1, source_target_pairs={{0,4},{4,8},{8,12},{12,16},{16,20},{20,24},{24,28},{1,5},{5,9},{9,... | collective-permute-start | bytes 491528 | tf_op jit(solution)/shard_map/ppermute | solution.py:18
  113.8 4.3 %collective-permute-done.11 = f32[4,2,1,5,4,256]{5,3,4,2,1,0:T(8,128)S(1)} collective-permute-done((f32[4,2,1,5,4,256]{5,3,4,2,1,0:T(8,128)S(1)}, f32[4,2,1,5,4,256]{5,3,4,2,1,0:T(8,128)S(1)}, u32[]{:S(2)}, u32[]{:S(2)}) %collective-permute-start.11) | collective-permute-done | bytes 163872 | tf_op jit(solution)/shard_map/ppermute | solution.py:19
  118.1 5.8 %collective-permute-done.10 = f32[4,2,1,5,4,256]{5,3,4,2,1,0:T(8,128)S(1)} collective-permute-done((f32[4,2,1,5,4,256]{5,3,4,2,1,0:T(8,128)S(1)}, f32[4,2,1,5,4,256]{5,3,4,2,1,0:T(8,128)S(1)}, u32[]{:S(2)}, u32[]{:S(2)}) %collective-permute-start.10) | collective-permute-done | bytes 163872 | tf_op jit(solution)/shard_map/ppermute | solution.py:18
  129.0 5.2 %collective-permute-start.12 = (f32[4,2,1,5,4,256]{5,3,4,2,1,0:T(8,128)S(1)}, f32[4,2,1,5,4,256]{5,3,4,2,1,0:T(8,128)S(1)}, u32[]{:S(2)}, u32[]{:S(2)}) collective-permute-start(f32[4,2,1,5,4,256]{5,3,4,2,1,0:T(8,128)S(1)} %get-tuple-element.43), channel_id=1, source_target_pairs={{0,4},{4,8},{8,12},{12,16},{16,20},{20,24},{24,28},{1,5},{5,9},{9,... | collective-permute-start | bytes 491528 | tf_op jit(solution)/shard_map/ppermute | solution.py:18
  138.6 5.8 %collective-permute-done.12 = f32[4,2,1,5,4,256]{5,3,4,2,1,0:T(8,128)S(1)} collective-permute-done((f32[4,2,1,5,4,256]{5,3,4,2,1,0:T(8,128)S(1)}, f32[4,2,1,5,4,256]{5,3,4,2,1,0:T(8,128)S(1)}, u32[]{:S(2)}, u32[]{:S(2)}) %collective-permute-start.12) | collective-permute-done | bytes 163872 | tf_op jit(solution)/shard_map/ppermute | solution.py:18
  149.5 5.0 %collective-permute-start.14 = (f32[4,2,1,5,4,256]{5,3,4,2,1,0:T(8,128)S(1)}, f32[4,2,1,5,4,256]{5,3,4,2,1,0:T(8,128)S(1)}, u32[]{:S(2)}, u32[]{:S(2)}) collective-permute-start(f32[4,2,1,5,4,256]{5,3,4,2,1,0:T(8,128)S(1)} %get-tuple-element.35), channel_id=1, source_target_pairs={{0,4},{4,8},{8,12},{12,16},{16,20},{20,24},{24,28},{1,5},{5,9},{9,... | collective-permute-start | bytes 491528 | tf_op jit(solution)/shard_map/ppermute | solution.py:18
  154.8 4.3 %collective-permute-done.15 = f32[4,2,1,5,4,256]{5,3,4,2,1,0:T(8,128)S(1)} collective-permute-done((f32[4,2,1,5,4,256]{5,3,4,2,1,0:T(8,128)S(1)}, f32[4,2,1,5,4,256]{5,3,4,2,1,0:T(8,128)S(1)}, u32[]{:S(2)}, u32[]{:S(2)}) %collective-permute-start.15) | collective-permute-done | bytes 163872 | tf_op jit(solution)/shard_map/ppermute | solution.py:19
  159.1 5.8 %collective-permute-done.14 = f32[4,2,1,5,4,256]{5,3,4,2,1,0:T(8,128)S(1)} collective-permute-done((f32[4,2,1,5,4,256]{5,3,4,2,1,0:T(8,128)S(1)}, f32[4,2,1,5,4,256]{5,3,4,2,1,0:T(8,128)S(1)}, u32[]{:S(2)}, u32[]{:S(2)}) %collective-permute-start.14) | collective-permute-done | bytes 163872 | tf_op jit(solution)/shard_map/ppermute | solution.py:18
  168.9 12.8 %all_to_all.33 = f32[4,2,4,5,4,256]{5,2,3,1,0,4:T(4,128)S(1)} all-to-all(f32[4,2,4,5,4,256]{5,2,3,1,0,4:T(4,128)S(1)} %copy.46), channel_id=1, replica_groups=mesh['gx'=8,'af'=4] {'af'}, dimensions={4} | all-to-all | bytes 1310720 | tf_op jit(solution)/shard_map/all_to_all | solution.py:64
  183.1 5.9 %psum.14 = f32[16,16]{0,1:T(8,128)S(1)} all-reduce(f32[16,16]{0,1:T(8,128)S(1)} %fusion.105), channel_id=1, replica_groups=mesh['gx'=8,'af'=4] {'af'}, use_global_device_ids=true, to_apply=%region_0.1 | all-reduce | flops 256 | bytes 2048 | tf_op jit(solution)/shard_map/psum | solution.py:68
  189.0 20.1 %psum.15 = f32[16,16]{0,1:T(8,128)S(1)} all-reduce(f32[16,16]{0,1:T(8,128)S(1)} %psum.14), channel_id=1, replica_groups=mesh['gx'=8,'af'=4] {'gx'}, use_global_device_ids=true, to_apply=%region_1.2 | all-reduce | flops 256 | bytes 2048 | tf_op jit(solution)/shard_map/psum | solution.py:69
  219.7 9.5 %all-to-all-done.1 = f32[16,2,4,5,1,256]{5,2,4,3,1,0:T(4,128)S(1)} async-done(((f32[16,2,4,5,1,256]{5,2,4,3,1,0:T(4,128)}), f32[16,2,4,5,1,256]{5,2,4,3,1,0:T(4,128)S(1)}, u32[]{:S(2)}, u32[]{:S(2)}) %all-to-all-start.1) | async-done | bytes 655392 | tf_op jit(solution)/shard_map/all_to_all | solution.py:73
  (104 shorter events, 76.3 us)
Async XLA Ops:
  0.6 4.7 %copy-start = (f32[5,5]{1,0:T(8,128)S(1)}, f32[5,5]{1,0:T(8,128)}, u32[]{:S(2)}) copy-start(f32[5,5]{1,0:T(8,128)} %param.8) | copy-start | bytes 304
  6.5 11.2 %collective-permute-start.1 = (f32[4,2,1,5,4,256]{5,3,4,2,1,0:T(8,128)S(1)}, f32[4,2,1,5,4,256]{5,3,4,2,1,0:T(8,128)S(1)}, u32[]{:S(2)}, u32[]{:S(2)}) collective-permute-start(f32[4,2,1,5,4,256]{5,3,4,2,1,0:T(8,128)S(1)} %get-tuple-element.88), channel_id=1, source_target_pairs={{4,0},{8,4},{12,8},{16,12},{20,16},{24,20},{28,24},{5,1},{9,5},{13... | collective-permute-start | bytes 491528 | tf_op jit(solution)/shard_map/ppermute | solution.py:19
  7.8 15.6 %collective-permute-start = (f32[4,2,1,5,4,256]{5,3,4,2,1,0:T(8,128)S(1)}, f32[4,2,1,5,4,256]{5,3,4,2,1,0:T(8,128)S(1)}, u32[]{:S(2)}, u32[]{:S(2)}) collective-permute-start(f32[4,2,1,5,4,256]{5,3,4,2,1,0:T(8,128)S(1)} %get-tuple-element.89), channel_id=1, source_target_pairs={{0,4},{4,8},{8,12},{12,16},{16,20},{20,24},{24,28},{1,5},{5,9},{9,... | collective-permute-start | bytes 491528 | tf_op jit(solution)/shard_map/ppermute | solution.py:18
  13.4 0.7 copy-start.2
  14.1 9.3 %copy-start.1 = (f32[4,2,4,5,4,256]{5,4,3,2,1,0:T(4,128)S(1)}, f32[4,2,4,5,4,256]{5,4,3,2,1,0:T(4,128)}, u32[]{:S(2)}) copy-start(f32[4,2,4,5,4,256]{5,4,3,2,1,0:T(4,128)} %param.5) | copy-start | bytes 1966084
  14.1 9.3 %copy-start.3 = (f32[4,4,256]{2,1,0:T(4,128)S(1)}, f32[4,4,256]{2,1,0:T(4,128)}, u32[]{:S(2)}) copy-start(f32[4,4,256]{2,1,0:T(4,128)} %param.7) | copy-start | bytes 49156
  26.6 10.9 %collective-permute-start.3 = (f32[4,2,1,5,4,256]{5,3,4,2,1,0:T(8,128)S(1)}, f32[4,2,1,5,4,256]{5,3,4,2,1,0:T(8,128)S(1)}, u32[]{:S(2)}, u32[]{:S(2)}) collective-permute-start(f32[4,2,1,5,4,256]{5,3,4,2,1,0:T(8,128)S(1)} %get-tuple-element.82), channel_id=1, source_target_pairs={{4,0},{8,4},{12,8},{16,12},{20,16},{24,20},{28,24},{5,1},{9,5},{13... | collective-permute-start | bytes 491528 | tf_op jit(solution)/shard_map/ppermute | solution.py:19
  27.9 15.3 %collective-permute-start.2 = (f32[4,2,1,5,4,256]{5,3,4,2,1,0:T(8,128)S(1)}, f32[4,2,1,5,4,256]{5,3,4,2,1,0:T(8,128)S(1)}, u32[]{:S(2)}, u32[]{:S(2)}) collective-permute-start(f32[4,2,1,5,4,256]{5,3,4,2,1,0:T(8,128)S(1)} %get-tuple-element.83), channel_id=1, source_target_pairs={{0,4},{4,8},{8,12},{12,16},{16,20},{20,24},{24,28},{1,5},{5,9},{9,... | collective-permute-start | bytes 491528 | tf_op jit(solution)/shard_map/ppermute | solution.py:18
  46.6 10.9 %collective-permute-start.5 = (f32[4,2,1,5,4,256]{5,3,4,2,1,0:T(8,128)S(1)}, f32[4,2,1,5,4,256]{5,3,4,2,1,0:T(8,128)S(1)}, u32[]{:S(2)}, u32[]{:S(2)}) collective-permute-start(f32[4,2,1,5,4,256]{5,3,4,2,1,0:T(8,128)S(1)} %get-tuple-element.74), channel_id=1, source_target_pairs={{4,0},{8,4},{12,8},{16,12},{20,16},{24,20},{28,24},{5,1},{9,5},{13... | collective-permute-start | bytes 491528 | tf_op jit(solution)/shard_map/ppermute | solution.py:19
  47.9 15.3 %collective-permute-start.4 = (f32[4,2,1,5,4,256]{5,3,4,2,1,0:T(8,128)S(1)}, f32[4,2,1,5,4,256]{5,3,4,2,1,0:T(8,128)S(1)}, u32[]{:S(2)}, u32[]{:S(2)}) collective-permute-start(f32[4,2,1,5,4,256]{5,3,4,2,1,0:T(8,128)S(1)} %get-tuple-element.75), channel_id=1, source_target_pairs={{0,4},{4,8},{8,12},{12,16},{16,20},{20,24},{24,28},{1,5},{5,9},{9,... | collective-permute-start | bytes 491528 | tf_op jit(solution)/shard_map/ppermute | solution.py:18
  66.7 10.9 %collective-permute-start.7 = (f32[4,2,1,5,4,256]{5,3,4,2,1,0:T(8,128)S(1)}, f32[4,2,1,5,4,256]{5,3,4,2,1,0:T(8,128)S(1)}, u32[]{:S(2)}, u32[]{:S(2)}) collective-permute-start(f32[4,2,1,5,4,256]{5,3,4,2,1,0:T(8,128)S(1)} %get-tuple-element.66), channel_id=1, source_target_pairs={{4,0},{8,4},{12,8},{16,12},{20,16},{24,20},{28,24},{5,1},{9,5},{13... | collective-permute-start | bytes 491528 | tf_op jit(solution)/shard_map/ppermute | solution.py:19
  68.0 15.3 %collective-permute-start.6 = (f32[4,2,1,5,4,256]{5,3,4,2,1,0:T(8,128)S(1)}, f32[4,2,1,5,4,256]{5,3,4,2,1,0:T(8,128)S(1)}, u32[]{:S(2)}, u32[]{:S(2)}) collective-permute-start(f32[4,2,1,5,4,256]{5,3,4,2,1,0:T(8,128)S(1)} %get-tuple-element.67), channel_id=1, source_target_pairs={{0,4},{4,8},{8,12},{12,16},{16,20},{20,24},{24,28},{1,5},{5,9},{9,... | collective-permute-start | bytes 491528 | tf_op jit(solution)/shard_map/ppermute | solution.py:18
  86.9 10.9 %collective-permute-start.9 = (f32[4,2,1,5,4,256]{5,3,4,2,1,0:T(8,128)S(1)}, f32[4,2,1,5,4,256]{5,3,4,2,1,0:T(8,128)S(1)}, u32[]{:S(2)}, u32[]{:S(2)}) collective-permute-start(f32[4,2,1,5,4,256]{5,3,4,2,1,0:T(8,128)S(1)} %get-tuple-element.58), channel_id=1, source_target_pairs={{4,0},{8,4},{12,8},{16,12},{20,16},{24,20},{28,24},{5,1},{9,5},{13... | collective-permute-start | bytes 491528 | tf_op jit(solution)/shard_map/ppermute | solution.py:19
  88.2 15.3 %collective-permute-start.8 = (f32[4,2,1,5,4,256]{5,3,4,2,1,0:T(8,128)S(1)}, f32[4,2,1,5,4,256]{5,3,4,2,1,0:T(8,128)S(1)}, u32[]{:S(2)}, u32[]{:S(2)}) collective-permute-start(f32[4,2,1,5,4,256]{5,3,4,2,1,0:T(8,128)S(1)} %get-tuple-element.59), channel_id=1, source_target_pairs={{0,4},{4,8},{8,12},{12,16},{16,20},{20,24},{24,28},{1,5},{5,9},{9,... | collective-permute-start | bytes 491528 | tf_op jit(solution)/shard_map/ppermute | solution.py:18
  107.3 10.9 %collective-permute-start.11 = (f32[4,2,1,5,4,256]{5,3,4,2,1,0:T(8,128)S(1)}, f32[4,2,1,5,4,256]{5,3,4,2,1,0:T(8,128)S(1)}, u32[]{:S(2)}, u32[]{:S(2)}) collective-permute-start(f32[4,2,1,5,4,256]{5,3,4,2,1,0:T(8,128)S(1)} %get-tuple-element.50), channel_id=1, source_target_pairs={{4,0},{8,4},{12,8},{16,12},{20,16},{24,20},{28,24},{5,1},{9,5},{13... | collective-permute-start | bytes 491528 | tf_op jit(solution)/shard_map/ppermute | solution.py:19
  108.6 15.3 %collective-permute-start.10 = (f32[4,2,1,5,4,256]{5,3,4,2,1,0:T(8,128)S(1)}, f32[4,2,1,5,4,256]{5,3,4,2,1,0:T(8,128)S(1)}, u32[]{:S(2)}, u32[]{:S(2)}) collective-permute-start(f32[4,2,1,5,4,256]{5,3,4,2,1,0:T(8,128)S(1)} %get-tuple-element.51), channel_id=1, source_target_pairs={{0,4},{4,8},{8,12},{12,16},{16,20},{20,24},{24,28},{1,5},{5,9},{9,... | collective-permute-start | bytes 491528 | tf_op jit(solution)/shard_map/ppermute | solution.py:18
  127.7 10.9 %collective-permute-start.13 = (f32[4,2,1,5,4,256]{5,3,4,2,1,0:T(8,128)S(1)}, f32[4,2,1,5,4,256]{5,3,4,2,1,0:T(8,128)S(1)}, u32[]{:S(2)}, u32[]{:S(2)}) collective-permute-start(f32[4,2,1,5,4,256]{5,3,4,2,1,0:T(8,128)S(1)} %get-tuple-element.42), channel_id=1, source_target_pairs={{4,0},{8,4},{12,8},{16,12},{20,16},{24,20},{28,24},{5,1},{9,5},{13... | collective-permute-start | bytes 491528 | tf_op jit(solution)/shard_map/ppermute | solution.py:19
  129.0 15.3 %collective-permute-start.12 = (f32[4,2,1,5,4,256]{5,3,4,2,1,0:T(8,128)S(1)}, f32[4,2,1,5,4,256]{5,3,4,2,1,0:T(8,128)S(1)}, u32[]{:S(2)}, u32[]{:S(2)}) collective-permute-start(f32[4,2,1,5,4,256]{5,3,4,2,1,0:T(8,128)S(1)} %get-tuple-element.43), channel_id=1, source_target_pairs={{0,4},{4,8},{8,12},{12,16},{16,20},{20,24},{24,28},{1,5},{5,9},{9,... | collective-permute-start | bytes 491528 | tf_op jit(solution)/shard_map/ppermute | solution.py:18
  148.2 10.9 %collective-permute-start.15 = (f32[4,2,1,5,4,256]{5,3,4,2,1,0:T(8,128)S(1)}, f32[4,2,1,5,4,256]{5,3,4,2,1,0:T(8,128)S(1)}, u32[]{:S(2)}, u32[]{:S(2)}) collective-permute-start(f32[4,2,1,5,4,256]{5,3,4,2,1,0:T(8,128)S(1)} %get-tuple-element.34), channel_id=1, source_target_pairs={{4,0},{8,4},{12,8},{16,12},{20,16},{24,20},{28,24},{5,1},{9,5},{13... | collective-permute-start | bytes 491528 | tf_op jit(solution)/shard_map/ppermute | solution.py:19
  149.5 15.3 %collective-permute-start.14 = (f32[4,2,1,5,4,256]{5,3,4,2,1,0:T(8,128)S(1)}, f32[4,2,1,5,4,256]{5,3,4,2,1,0:T(8,128)S(1)}, u32[]{:S(2)}, u32[]{:S(2)}) collective-permute-start(f32[4,2,1,5,4,256]{5,3,4,2,1,0:T(8,128)S(1)} %get-tuple-element.35), channel_id=1, source_target_pairs={{0,4},{4,8},{8,12},{12,16},{16,20},{20,24},{24,28},{1,5},{5,9},{9,... | collective-permute-start | bytes 491528 | tf_op jit(solution)/shard_map/ppermute | solution.py:18
  215.5 13.7 %all-to-all-start.1 = ((f32[16,2,4,5,1,256]{5,2,4,3,1,0:T(4,128)}), f32[16,2,4,5,1,256]{5,2,4,3,1,0:T(4,128)S(1)}, u32[]{:S(2)}, u32[]{:S(2)}) async-start(f32[16,2,4,5,1,256]{5,2,4,3,1,0:T(4,128)} %copy.50), calls=%async_computation.1 | async-start | bytes 1310720 | tf_op jit(solution)/shard_map/all_to_all | solution.py:73
where the time goes:
time: 231 us; the launch traced here: 230 us
  waiting for transfers between devices  88.6 us (38%)
  starting transfers between devices  54.9 us (24%)
  blocking collectives  38.7 us (17%)
  matrix products  18.3 us (8%)
  other arithmetic  16 us (7%)
  local copies, waits for them, and re-layouts  12.5 us (5%)
    ppermute x8, waiting for transfers between devices, padded_2(): before = lax.ppermute(last, axis, up)  46.1 us
    ppermute x8, starting transfers between devices, padded_2(): before = lax.ppermute(last, axis, up)  41.1 us
    ppermute x8, waiting for transfers between devices, padded_2(): after = lax.ppermute(leading, axis, down)  33 us
    psum x1, blocking collectives, on_device(): gram = lax.psum(partial_gram, 'gx')  20.1 us
    dot_general x8, matrix products, apply_adjoint(): jnp.einsum('wv,kpxwrt->kpxvrt', coupling, field, precision=lax.Precision....  16.5 us
    all_to_all x1, blocking collectives, on_device(): lax.all_to_all(field, 'af', split_axis=4, concat_axis=0, tiled=True)  12.8 us
    ppermute x8, starting transfers between devices, padded_2(): after = lax.ppermute(leading, axis, down)  10.3 us
    all_to_all x1, waiting for transfers between devices, on_device(): lax.all_to_all(scaled.reshape(regrouped.shape), 'af', split_axis=0, conca...  9.51 us
  transfers between devices with their start and end apart: 17, of which 17 were waited for; matrix products, arithmetic and copies ran while one was open for 1% of the time, Pallas kernels for 0%

commit v1 on v0

--- a/solution.py
+++ b/solution.py
@@ -66,7 +66,7 @@
     total = flat.shape[1] * lax.axis_size("gx") * lax.axis_size("af")
     local_gram = jnp.dot(flat, flat.T, precision=lax.Precision.HIGHEST)
     partial_gram = lax.psum(local_gram, "af")
-    gram = lax.psum(partial_gram, "gx")
+    gram = jnp.sum(lax.all_gather(partial_gram, "gx"), axis=0)
     lower_factor = jnp.linalg.cholesky(gram)
     inverse = jax.scipy.linalg.solve_triangular(lower_factor, eye_matrix, lower=True)
     scaled = jnp.dot(inverse, flat, precision=lax.Precision.HIGHEST) * jnp.sqrt(jnp.float32(total))

time: 231 us -> 242 us (1.048)
  blocking collectives: 38.7 us -> 49.2 us
    all_gather x0 -> x1, blocking collectives: none -> 30.5 us  [on_device(): gram = jnp.sum(lax.all_gather(partial_gram, 'gx'), axis=0)]
    psum x1 -> x0, blocking collectives: 20.1 us -> none  [on_device(): gram = lax.psum(partial_gram, 'gx')]
where the time goes in v1:
time: 242 us; the launch traced here: 241 us
  waiting for transfers between devices  88.6 us (37%)
  starting transfers between devices  54.9 us (23%)
  blocking collectives  49.2 us (20%)
  matrix products  18.3 us (8%)
  other arithmetic  16 us (7%)
  local copies, waits for them, and re-layouts  12.5 us (5%)
    ppermute x8, waiting for transfers between devices, padded_2(): before = lax.ppermute(last, axis, up)  46.1 us
    ppermute x8, starting transfers between devices, padded_2(): before = lax.ppermute(last, axis, up)  41.1 us
    ppermute x8, waiting for transfers between devices, padded_2(): after = lax.ppermute(leading, axis, down)  33 us
    all_gather x1, blocking collectives, on_device(): gram = jnp.sum(lax.all_gather(partial_gram, 'gx'), axis=0)  30.5 us
    dot_general x8, matrix products, apply_adjoint(): jnp.einsum('wv,kpxwrt->kpxvrt', coupling, field, precision=lax.Precision....  16.5 us
    all_to_all x1, blocking collectives, on_device(): lax.all_to_all(field, 'af', split_axis=4, concat_axis=0, tiled=True)  12.8 us
    ppermute x8, starting transfers between devices, padded_2(): after = lax.ppermute(leading, axis, down)  10.3 us
    all_to_all x1, waiting for transfers between devices, on_device(): lax.all_to_all(scaled.reshape(regrouped.shape), 'af', split_axis=0, conca...  9.51 us
  transfers between devices with their start and end apart: 17, of which 17 were waited for; matrix products, arithmetic and copies ran while one was open for 1% of the time, Pallas kernels for 0%

profile of v1, /device:TPU:0, one launch (start us, length us, event | category | flops | bytes accessed | tf_op | source)
XLA Modules:
  0.0 241.0 jit_solution(3952928435671190027)
XLA Ops:
  7.8 5.5 %collective-permute-start = (f32[4,2,1,5,4,256]{5,3,4,2,1,0:T(8,128)S(1)}, f32[4,2,1,5,4,256]{5,3,4,2,1,0:T(8,128)S(1)}, u32[]{:S(2)}, u32[]{:S(2)}) collective-permute-start(f32[4,2,1,5,4,256]{5,3,4,2,1,0:T(8,128)S(1)} %get-tuple-element.89), channel_id=1, source_target_pairs={{0,4},{4,8},{8,12},{12,16},{16,20},{20,24},{24,28},{1,5},{5,9},{9,... | collective-permute-start | bytes 491528 | tf_op jit(solution)/shard_map/ppermute | solution.py:18
  17.6 5.8 %collective-permute-done = f32[4,2,1,5,4,256]{5,3,4,2,1,0:T(8,128)S(1)} collective-permute-done((f32[4,2,1,5,4,256]{5,3,4,2,1,0:T(8,128)S(1)}, f32[4,2,1,5,4,256]{5,3,4,2,1,0:T(8,128)S(1)}, u32[]{:S(2)}, u32[]{:S(2)}) %collective-permute-start) | collective-permute-done | bytes 163872 | tf_op jit(solution)/shard_map/ppermute | solution.py:18
  27.9 5.0 %collective-permute-start.2 = (f32[4,2,1,5,4,256]{5,3,4,2,1,0:T(8,128)S(1)}, f32[4,2,1,5,4,256]{5,3,4,2,1,0:T(8,128)S(1)}, u32[]{:S(2)}, u32[]{:S(2)}) collective-permute-start(f32[4,2,1,5,4,256]{5,3,4,2,1,0:T(8,128)S(1)} %get-tuple-element.83), channel_id=1, source_target_pairs={{0,4},{4,8},{8,12},{12,16},{16,20},{20,24},{24,28},{1,5},{5,9},{9,... | collective-permute-start | bytes 491528 | tf_op jit(solution)/shard_map/ppermute | solution.py:18
  37.5 5.8 %collective-permute-done.2 = f32[4,2,1,5,4,256]{5,3,4,2,1,0:T(8,128)S(1)} collective-permute-done((f32[4,2,1,5,4,256]{5,3,4,2,1,0:T(8,128)S(1)}, f32[4,2,1,5,4,256]{5,3,4,2,1,0:T(8,128)S(1)}, u32[]{:S(2)}, u32[]{:S(2)}) %collective-permute-start.2) | collective-permute-done | bytes 163872 | tf_op jit(solution)/shard_map/ppermute | solution.py:18
  47.9 5.0 %collective-permute-start.4 = (f32[4,2,1,5,4,256]{5,3,4,2,1,0:T(8,128)S(1)}, f32[4,2,1,5,4,256]{5,3,4,2,1,0:T(8,128)S(1)}, u32[]{:S(2)}, u32[]{:S(2)}) collective-permute-start(f32[4,2,1,5,4,256]{5,3,4,2,1,0:T(8,128)S(1)} %get-tuple-element.75), channel_id=1, source_target_pairs={{0,4},{4,8},{8,12},{12,16},{16,20},{20,24},{24,28},{1,5},{5,9},{9,... | collective-permute-start | bytes 491528 | tf_op jit(solution)/shard_map/ppermute | solution.py:18
  53.1 4.3 %collective-permute-done.5 = f32[4,2,1,5,4,256]{5,3,4,2,1,0:T(8,128)S(1)} collective-permute-done((f32[4,2,1,5,4,256]{5,3,4,2,1,0:T(8,128)S(1)}, f32[4,2,1,5,4,256]{5,3,4,2,1,0:T(8,128)S(1)}, u32[]{:S(2)}, u32[]{:S(2)}) %collective-permute-start.5) | collective-permute-done | bytes 163872 | tf_op jit(solution)/shard_map/ppermute | solution.py:19
  57.5 5.8 %collective-permute-done.4 = f32[4,2,1,5,4,256]{5,3,4,2,1,0:T(8,128)S(1)} collective-permute-done((f32[4,2,1,5,4,256]{5,3,4,2,1,0:T(8,128)S(1)}, f32[4,2,1,5,4,256]{5,3,4,2,1,0:T(8,128)S(1)}, u32[]{:S(2)}, u32[]{:S(2)}) %collective-permute-start.4) | collective-permute-done | bytes 163872 | tf_op jit(solution)/shard_map/ppermute | solution.py:18
  68.0 5.2 %collective-permute-start.6 = (f32[4,2,1,5,4,256]{5,3,4,2,1,0:T(8,128)S(1)}, f32[4,2,1,5,4,256]{5,3,4,2,1,0:T(8,128)S(1)}, u32[]{:S(2)}, u32[]{:S(2)}) collective-permute-start(f32[4,2,1,5,4,256]{5,3,4,2,1,0:T(8,128)S(1)} %get-tuple-element.67), channel_id=1, source_target_pairs={{0,4},{4,8},{8,12},{12,16},{16,20},{20,24},{24,28},{1,5},{5,9},{9,... | collective-permute-start | bytes 491528 | tf_op jit(solution)/shard_map/ppermute | solution.py:18
  77.6 5.8 %collective-permute-done.6 = f32[4,2,1,5,4,256]{5,3,4,2,1,0:T(8,128)S(1)} collective-permute-done((f32[4,2,1,5,4,256]{5,3,4,2,1,0:T(8,128)S(1)}, f32[4,2,1,5,4,256]{5,3,4,2,1,0:T(8,128)S(1)}, u32[]{:S(2)}, u32[]{:S(2)}) %collective-permute-start.6) | collective-permute-done | bytes 163872 | tf_op jit(solution)/shard_map/ppermute | solution.py:18
  88.2 5.0 %collective-permute-start.8 = (f32[4,2,1,5,4,256]{5,3,4,2,1,0:T(8,128)S(1)}, f32[4,2,1,5,4,256]{5,3,4,2,1,0:T(8,128)S(1)}, u32[]{:S(2)}, u32[]{:S(2)}) collective-permute-start(f32[4,2,1,5,4,256]{5,3,4,2,1,0:T(8,128)S(1)} %get-tuple-element.59), channel_id=1, source_target_pairs={{0,4},{4,8},{8,12},{12,16},{16,20},{20,24},{24,28},{1,5},{5,9},{9,... | collective-permute-start | bytes 491528 | tf_op jit(solution)/shard_map/ppermute | solution.py:18
  93.5 4.3 %collective-permute-done.9 = f32[4,2,1,5,4,256]{5,3,4,2,1,0:T(8,128)S(1)} collective-permute-done((f32[4,2,1,5,4,256]{5,3,4,2,1,0:T(8,128)S(1)}, f32[4,2,1,5,4,256]{5,3,4,2,1,0:T(8,128)S(1)}, u32[]{:S(2)}, u32[]{:S(2)}) %collective-permute-start.9) | collective-permute-done | bytes 163872 | tf_op jit(solution)/shard_map/ppermute | solution.py:19
  97.8 5.8 %collective-permute-done.8 = f32[4,2,1,5,4,256]{5,3,4,2,1,0:T(8,128)S(1)} collective-permute-done((f32[4,2,1,5,4,256]{5,3,4,2,1,0:T(8,128)S(1)}, f32[4,2,1,5,4,256]{5,3,4,2,1,0:T(8,128)S(1)}, u32[]{:S(2)}, u32[]{:S(2)}) %collective-permute-start.8) | collective-permute-done | bytes 163872 | tf_op jit(solution)/shard_map/ppermute | solution.py:18
  108.6 5.0 %collective-permute-start.10 = (f32[4,2,1,5,4,256]{5,3,4,2,1,0:T(8,128)S(1)}, f32[4,2,1,5,4,256]{5,3,4,2,1,0:T(8,128)S(1)}, u32[]{:S(2)}, u32[]{:S(2)}) collective-permute-start(f32[4,2,1,5,4,256]{5,3,4,2,1,0:T(8,128)S(1)} %get-tuple-element.51), channel_id=1, source_target_pairs={{0,4},{4,8},{8,12},{12,16},{16,20},{20,24},{24,28},{1,5},{5,9},{9,... | collective-permute-start | bytes 491528 | tf_op jit(solution)/shard_map/ppermute | solution.py:18
  113.8 4.3 %collective-permute-done.11 = f32[4,2,1,5,4,256]{5,3,4,2,1,0:T(8,128)S(1)} collective-permute-done((f32[4,2,1,5,4,256]{5,3,4,2,1,0:T(8,128)S(1)}, f32[4,2,1,5,4,256]{5,3,4,2,1,0:T(8,128)S(1)}, u32[]{:S(2)}, u32[]{:S(2)}) %collective-permute-start.11) | collective-permute-done | bytes 163872 | tf_op jit(solution)/shard_map/ppermute | solution.py:19
  118.1 5.8 %collective-permute-done.10 = f32[4,2,1,5,4,256]{5,3,4,2,1,0:T(8,128)S(1)} collective-permute-done((f32[4,2,1,5,4,256]{5,3,4,2,1,0:T(8,128)S(1)}, f32[4,2,1,5,4,256]{5,3,4,2,1,0:T(8,128)S(1)}, u32[]{:S(2)}, u32[]{:S(2)}) %collective-permute-start.10) | collective-permute-done | bytes 163872 | tf_op jit(solution)/shard_map/ppermute | solution.py:18
  129.0 5.2 %collective-permute-start.12 = (f32[4,2,1,5,4,256]{5,3,4,2,1,0:T(8,128)S(1)}, f32[4,2,1,5,4,256]{5,3,4,2,1,0:T(8,128)S(1)}, u32[]{:S(2)}, u32[]{:S(2)}) collective-permute-start(f32[4,2,1,5,4,256]{5,3,4,2,1,0:T(8,128)S(1)} %get-tuple-element.43), channel_id=1, source_target_pairs={{0,4},{4,8},{8,12},{12,16},{16,20},{20,24},{24,28},{1,5},{5,9},{9,... | collective-permute-start | bytes 491528 | tf_op jit(solution)/shard_map/ppermute | solution.py:18
  138.6 5.8 %collective-permute-done.12 = f32[4,2,1,5,4,256]{5,3,4,2,1,0:T(8,128)S(1)} collective-permute-done((f32[4,2,1,5,4,256]{5,3,4,2,1,0:T(8,128)S(1)}, f32[4,2,1,5,4,256]{5,3,4,2,1,0:T(8,128)S(1)}, u32[]{:S(2)}, u32[]{:S(2)}) %collective-permute-start.12) | collective-permute-done | bytes 163872 | tf_op jit(solution)/shard_map/ppermute | solution.py:18
  149.5 5.0 %collective-permute-start.14 = (f32[4,2,1,5,4,256]{5,3,4,2,1,0:T(8,128)S(1)}, f32[4,2,1,5,4,256]{5,3,4,2,1,0:T(8,128)S(1)}, u32[]{:S(2)}, u32[]{:S(2)}) collective-permute-start(f32[4,2,1,5,4,256]{5,3,4,2,1,0:T(8,128)S(1)} %get-tuple-element.35), channel_id=1, source_target_pairs={{0,4},{4,8},{8,12},{12,16},{16,20},{20,24},{24,28},{1,5},{5,9},{9,... | collective-permute-start | bytes 491528 | tf_op jit(solution)/shard_map/ppermute | solution.py:18
  154.8 4.3 %collective-permute-done.15 = f32[4,2,1,5,4,256]{5,3,4,2,1,0:T(8,128)S(1)} collective-permute-done((f32[4,2,1,5,4,256]{5,3,4,2,1,0:T(8,128)S(1)}, f32[4,2,1,5,4,256]{5,3,4,2,1,0:T(8,128)S(1)}, u32[]{:S(2)}, u32[]{:S(2)}) %collective-permute-start.15) | collective-permute-done | bytes 163872 | tf_op jit(solution)/shard_map/ppermute | solution.py:19
  159.1 5.8 %collective-permute-done.14 = f32[4,2,1,5,4,256]{5,3,4,2,1,0:T(8,128)S(1)} collective-permute-done((f32[4,2,1,5,4,256]{5,3,4,2,1,0:T(8,128)S(1)}, f32[4,2,1,5,4,256]{5,3,4,2,1,0:T(8,128)S(1)}, u32[]{:S(2)}, u32[]{:S(2)}) %collective-permute-start.14) | collective-permute-done | bytes 163872 | tf_op jit(solution)/shard_map/ppermute | solution.py:18
  168.9 12.8 %all_to_all.33 = f32[4,2,4,5,4,256]{5,2,3,1,0,4:T(4,128)S(1)} all-to-all(f32[4,2,4,5,4,256]{5,2,3,1,0,4:T(4,128)S(1)} %copy.44), channel_id=1, replica_groups=mesh['gx'=8,'af'=4] {'af'}, dimensions={4} | all-to-all | bytes 1310720 | tf_op jit(solution)/shard_map/all_to_all | solution.py:64
  183.2 5.9 %psum.7 = f32[1,16,16]{2,1,0:T(8,128)S(1)} all-reduce(f32[1,16,16]{2,1,0:T(8,128)S(1)} %convolution_bitcast_fusion.8), channel_id=1, replica_groups=mesh['gx'=8,'af'=4] {'af'}, use_global_device_ids=true, to_apply=%region_0.1 | all-reduce | flops 256 | bytes 2048 | tf_op jit(solution)/shard_map/psum | solution.py:68
  189.0 30.5 %all_gather.7 = f32[8,16,16]{2,1,0:T(8,128)S(1)} all-gather(f32[1,16,16]{2,1,0:T(8,128)S(1)} %psum.7), channel_id=1, replica_groups=mesh['gx'=8,'af'=4] {'gx'}, dimensions={0}, use_global_device_ids=true | all-gather | bytes 9216 | tf_op jit(solution)/shard_map/all_gather | solution.py:69
  230.2 9.5 %all-to-all-done.1 = f32[16,2,4,5,1,256]{5,2,4,3,1,0:T(4,128)S(1)} async-done(((f32[16,2,4,5,1,256]{5,2,4,3,1,0:T(4,128)}), f32[16,2,4,5,1,256]{5,2,4,3,1,0:T(4,128)S(1)}, u32[]{:S(2)}, u32[]{:S(2)}) %all-to-all-start.1) | async-done | bytes 655392 | tf_op jit(solution)/shard_map/all_to_all | solution.py:73
  (105 shorter events, 76.4 us)
Async XLA Ops:
  0.6 4.7 %copy-start = (f32[5,5]{1,0:T(8,128)S(1)}, f32[5,5]{1,0:T(8,128)}, u32[]{:S(2)}) copy-start(f32[5,5]{1,0:T(8,128)} %param.8) | copy-start | bytes 304
  6.5 11.2 %collective-permute-start.1 = (f32[4,2,1,5,4,256]{5,3,4,2,1,0:T(8,128)S(1)}, f32[4,2,1,5,4,256]{5,3,4,2,1,0:T(8,128)S(1)}, u32[]{:S(2)}, u32[]{:S(2)}) collective-permute-start(f32[4,2,1,5,4,256]{5,3,4,2,1,0:T(8,128)S(1)} %get-tuple-element.88), channel_id=1, source_target_pairs={{4,0},{8,4},{12,8},{16,12},{20,16},{24,20},{28,24},{5,1},{9,5},{13... | collective-permute-start | bytes 491528 | tf_op jit(solution)/shard_map/ppermute | solution.py:19
  7.8 15.6 %collective-permute-start = (f32[4,2,1,5,4,256]{5,3,4,2,1,0:T(8,128)S(1)}, f32[4,2,1,5,4,256]{5,3,4,2,1,0:T(8,128)S(1)}, u32[]{:S(2)}, u32[]{:S(2)}) collective-permute-start(f32[4,2,1,5,4,256]{5,3,4,2,1,0:T(8,128)S(1)} %get-tuple-element.89), channel_id=1, source_target_pairs={{0,4},{4,8},{8,12},{12,16},{16,20},{20,24},{24,28},{1,5},{5,9},{9,... | collective-permute-start | bytes 491528 | tf_op jit(solution)/shard_map/ppermute | solution.py:18
  13.4 0.7 copy-start.2
  14.1 9.3 %copy-start.1 = (f32[4,2,4,5,4,256]{5,4,3,2,1,0:T(4,128)S(1)}, f32[4,2,4,5,4,256]{5,4,3,2,1,0:T(4,128)}, u32[]{:S(2)}) copy-start(f32[4,2,4,5,4,256]{5,4,3,2,1,0:T(4,128)} %param.5) | copy-start | bytes 1966084
  14.1 9.3 %copy-start.3 = (f32[4,4,256]{2,1,0:T(4,128)S(1)}, f32[4,4,256]{2,1,0:T(4,128)}, u32[]{:S(2)}) copy-start(f32[4,4,256]{2,1,0:T(4,128)} %param.7) | copy-start | bytes 49156
  26.6 10.9 %collective-permute-start.3 = (f32[4,2,1,5,4,256]{5,3,4,2,1,0:T(8,128)S(1)}, f32[4,2,1,5,4,256]{5,3,4,2,1,0:T(8,128)S(1)}, u32[]{:S(2)}, u32[]{:S(2)}) collective-permute-start(f32[4,2,1,5,4,256]{5,3,4,2,1,0:T(8,128)S(1)} %get-tuple-element.82), channel_id=1, source_target_pairs={{4,0},{8,4},{12,8},{16,12},{20,16},{24,20},{28,24},{5,1},{9,5},{13... | collective-permute-start | bytes 491528 | tf_op jit(solution)/shard_map/ppermute | solution.py:19
  27.9 15.3 %collective-permute-start.2 = (f32[4,2,1,5,4,256]{5,3,4,2,1,0:T(8,128)S(1)}, f32[4,2,1,5,4,256]{5,3,4,2,1,0:T(8,128)S(1)}, u32[]{:S(2)}, u32[]{:S(2)}) collective-permute-start(f32[4,2,1,5,4,256]{5,3,4,2,1,0:T(8,128)S(1)} %get-tuple-element.83), channel_id=1, source_target_pairs={{0,4},{4,8},{8,12},{12,16},{16,20},{20,24},{24,28},{1,5},{5,9},{9,... | collective-permute-start | bytes 491528 | tf_op jit(solution)/shard_map/ppermute | solution.py:18
  46.6 10.9 %collective-permute-start.5 = (f32[4,2,1,5,4,256]{5,3,4,2,1,0:T(8,128)S(1)}, f32[4,2,1,5,4,256]{5,3,4,2,1,0:T(8,128)S(1)}, u32[]{:S(2)}, u32[]{:S(2)}) collective-permute-start(f32[4,2,1,5,4,256]{5,3,4,2,1,0:T(8,128)S(1)} %get-tuple-element.74), channel_id=1, source_target_pairs={{4,0},{8,4},{12,8},{16,12},{20,16},{24,20},{28,24},{5,1},{9,5},{13... | collective-permute-start | bytes 491528 | tf_op jit(solution)/shard_map/ppermute | solution.py:19
  47.9 15.3 %collective-permute-start.4 = (f32[4,2,1,5,4,256]{5,3,4,2,1,0:T(8,128)S(1)}, f32[4,2,1,5,4,256]{5,3,4,2,1,0:T(8,128)S(1)}, u32[]{:S(2)}, u32[]{:S(2)}) collective-permute-start(f32[4,2,1,5,4,256]{5,3,4,2,1,0:T(8,128)S(1)} %get-tuple-element.75), channel_id=1, source_target_pairs={{0,4},{4,8},{8,12},{12,16},{16,20},{20,24},{24,28},{1,5},{5,9},{9,... | collective-permute-start | bytes 491528 | tf_op jit(solution)/shard_map/ppermute | solution.py:18
  66.7 10.9 %collective-permute-start.7 = (f32[4,2,1,5,4,256]{5,3,4,2,1,0:T(8,128)S(1)}, f32[4,2,1,5,4,256]{5,3,4,2,1,0:T(8,128)S(1)}, u32[]{:S(2)}, u32[]{:S(2)}) collective-permute-start(f32[4,2,1,5,4,256]{5,3,4,2,1,0:T(8,128)S(1)} %get-tuple-element.66), channel_id=1, source_target_pairs={{4,0},{8,4},{12,8},{16,12},{20,16},{24,20},{28,24},{5,1},{9,5},{13... | collective-permute-start | bytes 491528 | tf_op jit(solution)/shard_map/ppermute | solution.py:19
  68.0 15.3 %collective-permute-start.6 = (f32[4,2,1,5,4,256]{5,3,4,2,1,0:T(8,128)S(1)}, f32[4,2,1,5,4,256]{5,3,4,2,1,0:T(8,128)S(1)}, u32[]{:S(2)}, u32[]{:S(2)}) collective-permute-start(f32[4,2,1,5,4,256]{5,3,4,2,1,0:T(8,128)S(1)} %get-tuple-element.67), channel_id=1, source_target_pairs={{0,4},{4,8},{8,12},{12,16},{16,20},{20,24},{24,28},{1,5},{5,9},{9,... | collective-permute-start | bytes 491528 | tf_op jit(solution)/shard_map/ppermute | solution.py:18
  86.9 10.9 %collective-permute-start.9 = (f32[4,2,1,5,4,256]{5,3,4,2,1,0:T(8,128)S(1)}, f32[4,2,1,5,4,256]{5,3,4,2,1,0:T(8,128)S(1)}, u32[]{:S(2)}, u32[]{:S(2)}) collective-permute-start(f32[4,2,1,5,4,256]{5,3,4,2,1,0:T(8,128)S(1)} %get-tuple-element.58), channel_id=1, source_target_pairs={{4,0},{8,4},{12,8},{16,12},{20,16},{24,20},{28,24},{5,1},{9,5},{13... | collective-permute-start | bytes 491528 | tf_op jit(solution)/shard_map/ppermute | solution.py:19
  88.2 15.3 %collective-permute-start.8 = (f32[4,2,1,5,4,256]{5,3,4,2,1,0:T(8,128)S(1)}, f32[4,2,1,5,4,256]{5,3,4,2,1,0:T(8,128)S(1)}, u32[]{:S(2)}, u32[]{:S(2)}) collective-permute-start(f32[4,2,1,5,4,256]{5,3,4,2,1,0:T(8,128)S(1)} %get-tuple-element.59), channel_id=1, source_target_pairs={{0,4},{4,8},{8,12},{12,16},{16,20},{20,24},{24,28},{1,5},{5,9},{9,... | collective-permute-start | bytes 491528 | tf_op jit(solution)/shard_map/ppermute | solution.py:18
  107.3 10.9 %collective-permute-start.11 = (f32[4,2,1,5,4,256]{5,3,4,2,1,0:T(8,128)S(1)}, f32[4,2,1,5,4,256]{5,3,4,2,1,0:T(8,128)S(1)}, u32[]{:S(2)}, u32[]{:S(2)}) collective-permute-start(f32[4,2,1,5,4,256]{5,3,4,2,1,0:T(8,128)S(1)} %get-tuple-element.50), channel_id=1, source_target_pairs={{4,0},{8,4},{12,8},{16,12},{20,16},{24,20},{28,24},{5,1},{9,5},{13... | collective-permute-start | bytes 491528 | tf_op jit(solution)/shard_map/ppermute | solution.py:19
  108.6 15.3 %collective-permute-start.10 = (f32[4,2,1,5,4,256]{5,3,4,2,1,0:T(8,128)S(1)}, f32[4,2,1,5,4,256]{5,3,4,2,1,0:T(8,128)S(1)}, u32[]{:S(2)}, u32[]{:S(2)}) collective-permute-start(f32[4,2,1,5,4,256]{5,3,4,2,1,0:T(8,128)S(1)} %get-tuple-element.51), channel_id=1, source_target_pairs={{0,4},{4,8},{8,12},{12,16},{16,20},{20,24},{24,28},{1,5},{5,9},{9,... | collective-permute-start | bytes 491528 | tf_op jit(solution)/shard_map/ppermute | solution.py:18
  127.7 10.9 %collective-permute-start.13 = (f32[4,2,1,5,4,256]{5,3,4,2,1,0:T(8,128)S(1)}, f32[4,2,1,5,4,256]{5,3,4,2,1,0:T(8,128)S(1)}, u32[]{:S(2)}, u32[]{:S(2)}) collective-permute-start(f32[4,2,1,5,4,256]{5,3,4,2,1,0:T(8,128)S(1)} %get-tuple-element.42), channel_id=1, source_target_pairs={{4,0},{8,4},{12,8},{16,12},{20,16},{24,20},{28,24},{5,1},{9,5},{13... | collective-permute-start | bytes 491528 | tf_op jit(solution)/shard_map/ppermute | solution.py:19
  129.0 15.3 %collective-permute-start.12 = (f32[4,2,1,5,4,256]{5,3,4,2,1,0:T(8,128)S(1)}, f32[4,2,1,5,4,256]{5,3,4,2,1,0:T(8,128)S(1)}, u32[]{:S(2)}, u32[]{:S(2)}) collective-permute-start(f32[4,2,1,5,4,256]{5,3,4,2,1,0:T(8,128)S(1)} %get-tuple-element.43), channel_id=1, source_target_pairs={{0,4},{4,8},{8,12},{12,16},{16,20},{20,24},{24,28},{1,5},{5,9},{9,... | collective-permute-start | bytes 491528 | tf_op jit(solution)/shard_map/ppermute | solution.py:18
  148.2 10.9 %collective-permute-start.15 = (f32[4,2,1,5,4,256]{5,3,4,2,1,0:T(8,128)S(1)}, f32[4,2,1,5,4,256]{5,3,4,2,1,0:T(8,128)S(1)}, u32[]{:S(2)}, u32[]{:S(2)}) collective-permute-start(f32[4,2,1,5,4,256]{5,3,4,2,1,0:T(8,128)S(1)} %get-tuple-element.34), channel_id=1, source_target_pairs={{4,0},{8,4},{12,8},{16,12},{20,16},{24,20},{28,24},{5,1},{9,5},{13... | collective-permute-start | bytes 491528 | tf_op jit(solution)/shard_map/ppermute | solution.py:19
  149.5 15.3 %collective-permute-start.14 = (f32[4,2,1,5,4,256]{5,3,4,2,1,0:T(8,128)S(1)}, f32[4,2,1,5,4,256]{5,3,4,2,1,0:T(8,128)S(1)}, u32[]{:S(2)}, u32[]{:S(2)}) collective-permute-start(f32[4,2,1,5,4,256]{5,3,4,2,1,0:T(8,128)S(1)} %get-tuple-element.35), channel_id=1, source_target_pairs={{0,4},{4,8},{8,12},{12,16},{16,20},{20,24},{24,28},{1,5},{5,9},{9,... | collective-permute-start | bytes 491528 | tf_op jit(solution)/shard_map/ppermute | solution.py:18
  226.0 13.7 %all-to-all-start.1 = ((f32[16,2,4,5,1,256]{5,2,4,3,1,0:T(4,128)}), f32[16,2,4,5,1,256]{5,2,4,3,1,0:T(4,128)S(1)}, u32[]{:S(2)}, u32[]{:S(2)}) async-start(f32[16,2,4,5,1,256]{5,2,4,3,1,0:T(4,128)} %copy.47), calls=%async_computation.1 | async-start | bytes 1310720 | tf_op jit(solution)/shard_map/all_to_all | solution.py:73
